TPU v7x, 128 devices: a whole 4x4x4 slice. The times are simulated.
128 devices in a mesh: dp: 2 (over core), space: 64 (over y, z, x).
Axes of the slice: x: 4, y: 4, z: 4, core: 2. Of those that a mesh axis runs over, the one named last changes fastest.
Arguments:
- features: bfloat16 [2, 4096, 16, 1024], P('dp', 'space'), may hold values from -6 to 6
- psi: bfloat16 [2, 4096, 64, 256], P('dp', 'space'), may hold values from -0.75 to 0.75
- neighbors: int32 [2, 4096, 16], P('dp', 'space'), may hold values from 0 to 4095, as said below
- counts: int32 [2, 4096], P('dp', 'space'), may hold values from 4 to 16, as said below
- occupation: float32 [2, 256], P('dp'), may hold values from 0.1 to 1
- weights: bfloat16 [1024, 4096], P(None, 'space'), may hold values from -0.1875 to 0.1875
Outputs:
- energies: float32 [2, 256], P('dp')
- gradient: float32 [4096, 1024], P('space')
Inputs may be any that keep to these rules, and one draw needn't show every extreme that they name: `neighbors`: every neighbor tile lies in the same cluster of 64 consecutive tiles or in one of the two clusters beside it, counted around a closed loop of 64 clusters. `counts`: the first tile of every twist uses all 16 slots.
All inputs are finite; a program needn't handle non-finite values.
Results may differ from a plain program's by a relative error of at most 0.004.
Values may be sent and summed in bfloat16 or wider, within the bound.
No kernel may reach another device: no remote copies, remote signals or barrier semaphores. Data moves between devices by JAX's collectives and lax.ppermute only.
A program may use at most 192 MiB of HBM per device.

v0:
```python
import math
import jax
import jax.numpy as jnp
from jax import lax
from jax.sharding import PartitionSpec as P


def with_halo(value, sides, width):
    for axis, dim in sides:
        size, length = (lax.axis_size(axis), value.shape[dim])
        up = [(i, (i + 1) % size) for i in range(size)]
        down = [(j, i) for i, j in up]
        last = lax.slice_in_dim(value, length - width, length, axis=dim)
        leading = lax.slice_in_dim(value, 0, width, axis=dim)
        before = lax.ppermute(last, axis, up)
        after = lax.ppermute(leading, axis, down)
        value = jnp.concatenate([before, value, after], axis=dim)
    return value


def local(features, psi, neighbors, counts, occupation, weights):
    twists_here, rows, slots, width = features.shape
    orbit = psi.shape[2]
    bands = psi.shape[3]
    nspace = lax.axis_size("space")
    myself = lax.axis_index("space")
    factor = 1.0 / math.sqrt(rows * nspace * slots)
    flat = features.reshape(twists_here * rows * slots, width)
    products = jnp.dot(
        flat,
        lax.all_gather(weights, "space", axis=1, tiled=True),
        preferred_element_type=jnp.float32,
    )
    valid = (
        lax.broadcasted_iota(jnp.int32, (twists_here, rows, slots), 2) < counts[:, :, None]
    ).astype(jnp.bfloat16)
    blocks = (
        products.astype(jnp.bfloat16).reshape(twists_here, rows, slots, orbit, orbit)
        * valid[:, :, :, None, None]
    )
    widened = with_halo(psi, (("space", 1),), rows)
    owners = neighbors // rows
    placed = (owners - myself + 1 + nspace) % nspace * rows + neighbors % rows
    weighted = (psi.astype(jnp.float32) * occupation[:, None, None, :]).astype(jnp.bfloat16)

    def per_slot(carry, inputs):
        block_k, index_k, valid_k = inputs
        fetched = jax.vmap(lambda table, where: table[where])(widened, index_k)
        carry = carry + jnp.einsum(
            "trac,trcb->trab", block_k, fetched, preferred_element_type=jnp.float32
        )
        grad_k = (
            factor
            * jnp.einsum("trab,trcb->trac", weighted, fetched, preferred_element_type=jnp.float32)
        ).astype(jnp.bfloat16)
        return (carry, grad_k * valid_k[:, :, None, None])

    inputs = (jnp.moveaxis(blocks, 2, 0), jnp.moveaxis(placed, 2, 0), jnp.moveaxis(valid, 2, 0))
    applied, dblocks = lax.scan(
        per_slot, jnp.zeros((twists_here, rows, orbit, bands), jnp.float32), inputs
    )
    partial_energy = factor * jnp.sum(psi.astype(jnp.float32) * applied, axis=(1, 2))
    energies = lax.psum(partial_energy, "space")
    square = orbit * orbit
    flat_grads = dblocks.reshape(slots, twists_here, rows, square)
    share = lax.psum_scatter(
        jnp.einsum("strO,trsf->Of", flat_grads, features, preferred_element_type=jnp.float32),
        "space",
        scatter_dimension=0,
        tiled=True,
    )
    gradient = lax.psum(share, "dp")
    return (energies, gradient)


def solution(mesh):
    placed = (
        P("dp", "space", None, None),
        P("dp", "space", None, None),
        P("dp", "space", None),
        P("dp", "space"),
        P("dp", None),
        P(None, "space"),
    )
    return jax.shard_map(
        local,
        mesh=mesh,
        in_specs=placed,
        out_specs=(P("dp", None), P("space", None)),
        check_vma=False,
    )
```

profile of v0, /device:TPU:0, one launch (start us, length us, event | category | flops | bytes accessed | tf_op | source)
XLA Modules:
  0.0 1062.5 jit_solution(6959014675251214178)
XLA Ops:
  9.6 7.3 collective-permute-start.1
  22.7 41.5 %collective-permute-done = bf16[1,64,64,256]{3,2,1,0:T(8,128)(2,1)} collective-permute-done((bf16[1,64,64,256]{3,2,1,0:T(8,128)(2,1)}, bf16[1,64,64,256]{3,2,1,0:T(8,128)(2,1)}, u32[]{:S(2)}, u32[]{:S(2)}) %collective-permute-start) | collective-permute-done | bytes 2097184 | tf_op jit(solution)/shard_map/ppermute | solution.py:15
  69.7 51.4 %all-gather.2.cloned.1.call-done = bf16[1024,4096]{0,1:T(8,128)(2,1)} async-done(((bf16[1024,64]{0,1:T(8,128)(2,1)}), bf16[1024,4096]{0,1:T(8,128)(2,1)}) %all-gather.2.cloned.1.call-update) | async-done | bytes 8388624 | tf_op jit(solution)/shard_map/all_gather | solution.py:31
  121.1 14.3 %convolution_convert_fusion = bf16[1024,4096]{1,0:T(8,128)(2,1)} fusion(bf16[1024,1024]{1,0:T(8,128)(2,1)S(1)} %bitcast.74, bf16[1024,4096]{0,1:T(8,128)(2,1)} %all-gather.2.cloned.1.call-done), kind=kOutput, calls=%fused_computation.21 | convolution fusion | flops 8594128896 | bytes 18874368 | tf_op jit(solution)/shard_map/dot_general | solution.py:29
  135.4 23.6 %reshape.163 = bf16[1,64,16,64,64]{4,3,2,1,0:T(8,128)(2,1)} reshape(bf16[1024,4096]{1,0:T(8,128)(2,1)} %convolution_convert_fusion) | data formatting | bytes 16777216 | tf_op jit(solution)/shard_map/reshape | solution.py:38
  159.0 14.0 %fusion.15 = bf16[16,1,64,64,64]{4,3,2,1,0:T(8,128)(2,1)} fusion(bf16[1,64,16,64,64]{4,3,2,1,0:T(8,128)(2,1)} %reshape.163, bf16[64,16]{0,1:T(8,128)(2,1)S(1)} %fusion.24), kind=kLoop, calls=%fused_computation.19 | loop fusion | flops 4194304 | bytes 16779264 | tf_op jit(solution)/shard_map/transpose | solution.py:58
  173.0 274.1 %while.13 = (s32[]{:T(128)}, f32[1,64,64,256]{3,2,1,0:T(8,128)}, bf16[16,1,64,64,64]{4,3,2,0,1:T(8,128)(2,1)}, bf16[16,1,64,64,64]{4,3,2,1,0:T(8,128)(2,1)}, s32...) while((s32[]{:T(128)}, f32[1,64,64,256]{3,2,1,0:T(8,128)}, ...), condition=%wide.region_1.2_spmd.clone, body=%wide.region_0.1_spmd.clone.sunk | while | flops 271319552 | bytes 23071752 | solution.py:59
  199.3 5.8 bitcast_add_fusion.2
  216.5 5.8 bitcast_add_fusion.2
  233.7 5.8 bitcast_add_fusion.2
  250.9 5.8 bitcast_add_fusion.2
  268.1 5.8 bitcast_add_fusion.2
  285.3 5.8 bitcast_add_fusion.2
  302.5 5.8 bitcast_add_fusion.2
  337.0 5.8 bitcast_add_fusion.2
  354.2 5.8 bitcast_add_fusion.2
  388.5 5.8 bitcast_add_fusion.2
  405.8 5.8 bitcast_add_fusion.2
  423.0 5.8 bitcast_add_fusion.2
  440.2 5.8 bitcast_add_fusion.2
  447.1 22.6 %reshape.164 = bf16[16,64,4096]{2,1,0:T(8,128)(2,1)} reshape(bf16[16,1,64,64,64]{4,3,2,0,1:T(8,128)(2,1)} %get-tuple-element.46) | data formatting | bytes 16777216 | tf_op jit(solution)/shard_map/reshape.16
  469.7 15.7 %convolution_bitcast_fusion = f32[4096,1024]{1,0:T(8,128)} fusion(bf16[16,64,4096]{2,1,0:T(8,128)(2,1)} %reshape.164, bf16[64,16,1024]{2,1,0:T(8,128)(2,1)S(1)} %bitcast.75), kind=kOutput, calls=%fused_computation.20 | convolution fusion | flops 8589934592 | bytes 27262976 | tf_op jit(solution)/shard_map/strO,trsf->Of/dot_general | solution.py:67
  485.4 392.0 %reduce-scatter.2.cloned.1.call-done = f32[64,1024]{1,0:T(8,128)} async-done(((f32[4096,1024]{1,0:T(8,128)}), f32[64,1024]{1,0:T(8,128)}) %reduce-scatter.2.cloned.1.call-update) | async-done | bytes 262160 | tf_op jit(solution)/shard_map/reduce_scatter | solution.py:66
  880.9 173.4 %psum.14 = f32[1,256]{1,0:T(1,128)} all-reduce(f32[1,256]{1,0:T(1,128)S(1)} %bitcast.77), channel_id=1, replica_groups=mesh['dp'=2,'space'=64] {'space'}, use_global_device_ids=true, to_apply=%region_3.4 | all-reduce | flops 256 | bytes 2048 | tf_op jit(solution)/shard_map/psum | solution.py:63
  (154 shorter events, 217.0 us)
Async XLA Ops:
  7.2 114.0 %copy-start = (bf16[1,64,16,1024]{3,2,1,0:T(8,128)(2,1)S(1)}, bf16[1,64,16,1024]{3,2,1,0:T(8,128)(2,1)}, u32[]{:S(2)}) copy-start(bf16[1,64,16,1024]{3,2,1,0:T(8,128)(2,1)} %param.8) | copy-start | bytes 6291460
  7.2 113.9 %all-gather.2.cloned.1.call-start = ((), (), s32[]{:S(2)}) async-start(), calls=%async_computation.1 | async-start | bytes 8519680 | tf_op jit(solution)/shard_map/all_gather | solution.py:31
  7.9 869.5 %reduce-scatter.2.cloned.1.call-start = ((), (), s32[]{:S(2)}) async-start(), calls=%async_computation.2 | async-start | bytes 17039360 | tf_op jit(solution)/shard_map/reduce_scatter | solution.py:66
  8.0 56.2 %collective-permute-start = (bf16[1,64,64,256]{3,2,1,0:T(8,128)(2,1)}, bf16[1,64,64,256]{3,2,1,0:T(8,128)(2,1)}, u32[]{:S(2)}, u32[]{:S(2)}) collective-permute-start(bf16[1,64,64,256]{3,2,1,0:T(8,128)(2,1)} %param.9), channel_id=1, source_target_pairs={{0,1},{1,2},{2,3},{3,4},{4,5},{5,6},{6,7},{7,8},{8,9},{9,10},{10,1... | collective-permute-start | bytes 6291464 | tf_op jit(solution)/shard_map/ppermute | solution.py:15
  9.6 54.6 %collective-permute-start.1 = (bf16[1,64,64,256]{3,2,1,0:T(8,128)(2,1)}, bf16[1,64,64,256]{3,2,1,0:T(8,128)(2,1)}, u32[]{:S(2)}, u32[]{:S(2)}) collective-permute-start(bf16[1,64,64,256]{3,2,1,0:T(8,128)(2,1)} %param.9), channel_id=1, source_target_pairs={{1,0},{2,1},{3,2},{4,3},{5,4},{6,5},{7,6},{8,7},{9,8},{10,9},{11,1... | collective-permute-start | bytes 6291464 | tf_op jit(solution)/shard_map/ppermute | solution.py:16
  16.9 47.3 %copy-start.1 = (bf16[1,64,64,256]{3,2,1,0:T(8,128)(2,1)S(1)}, bf16[1,64,64,256]{3,2,1,0:T(8,128)(2,1)}, u32[]{:S(2)}) copy-start(bf16[1,64,64,256]{3,2,1,0:T(8,128)(2,1)} %param.9) | copy-start | bytes 6291460
  485.4 568.9 %all-reduce.2.cloned.1.call-start = ((), (), s32[]{:S(2)}) async-start(), calls=%async_computation.3 | async-start | bytes 524288 | tf_op jit(solution)/shard_map/psum | solution.py:72
Sparse Core Ops, SparseCore 0:
  10.9 110.2 all-gather.1
  485.5 391.8 reduce-scatter.1
  879.8 18.4 all-reduce.1
where the time goes:
time: 1070 us; the launch traced here: 1060 us
  waiting for transfers between devices  486 us (45%)
  matrix products  184 us (17%)
  blocking collectives  173 us (16%)
  local copies, waits for them, and re-layouts  167 us (16%)
  other arithmetic  28.9 us (3%)
  between operations  13.8 us (1%)
    reduce_scatter x1, waiting for transfers between devices, local(): lax.psum_scatter(jnp.einsum('strO,trsf->Of', flat_grads, features, prefer...  392 us
    psum x1, blocking collectives, local(): energies = lax.psum(partial_energy, 'space')  173 us
    dot_general x16, matrix products, per_slot(): jnp.einsum('trac,trcb->trab', block_k, fetched, preferred_element_type=jn...  92 us
    gather x32, local copies, waits for them, and re-layouts, per_slot(): fetched = jax.vmap(lambda table, where: table[where])(widened, index_k)  76.5 us
    dot_general x16, matrix products, per_slot(): jnp.einsum('trab,trcb->trac', weighted, fetched, preferred_element_type=j...  62.4 us
    all_gather x1, waiting for transfers between devices, local(): lax.all_gather(weights, 'space', axis=1, tiled=True)  51.4 us
    dynamic_update_slice x32, local copies, waits for them, and re-layouts, local(): lax.scan(per_slot, jnp.zeros((twists_here, rows, orbit, bands), jnp.float...  42.7 us
    ppermute x1, waiting for transfers between devices, with_halo(): before = lax.ppermute(last, axis, up)  41.5 us
  transfers between devices with their start and end apart: 5, of which 3 were waited for; matrix products, arithmetic and copies ran while one was open for 1% of the time, Pallas kernels for 0%

commit v1 on v0

--- a/solution.py
+++ b/solution.py
@@ -60,7 +60,12 @@
         per_slot, jnp.zeros((twists_here, rows, orbit, bands), jnp.float32), inputs
     )
     partial_energy = factor * jnp.sum(psi.astype(jnp.float32) * applied, axis=(1, 2))
-    energies = lax.psum(partial_energy, "space")
+
+    def place_counts(local_x, axis_key):
+        side_arr = lax.all_gather(local_x, axis_name=axis_key)
+        return jnp.sum(side_arr, 0)
+
+    energies = place_counts(partial_energy, "space")
     square = orbit * orbit
     flat_grads = dblocks.reshape(slots, twists_here, rows, square)
     share = lax.psum_scatter(

time: 1070 us -> 1060 us (level)
    psum x1 -> x0, blocking collectives: 173 us -> none  [local(): energies = lax.psum(partial_energy, 'space')]
    all_gather x0 -> x1, blocking collectives: none -> 171 us  [place_counts(): side_arr = lax.all_gather(local_x, axis_name=axis_key)]
where the time goes in v1:
time: 1060 us
  waiting for transfers between devices  486 us (46%)
  matrix products  184 us (17%)
  blocking collectives  171 us (16%)
  local copies, waits for them, and re-layouts  167 us (16%)
  other arithmetic  29.6 us (3%)
  between operations  13.8 us (1%)
    reduce_scatter x1, waiting for transfers between devices, local(): lax.psum_scatter(jnp.einsum('strO,trsf->Of', flat_grads, features, prefer...  392 us
    all_gather x1, blocking collectives, place_counts(): side_arr = lax.all_gather(local_x, axis_name=axis_key)  171 us
    dot_general x16, matrix products, per_slot(): jnp.einsum('trac,trcb->trab', block_k, fetched, preferred_element_type=jn...  92 us
    gather x32, local copies, waits for them, and re-layouts, per_slot(): fetched = jax.vmap(lambda table, where: table[where])(widened, index_k)  76.5 us
    dot_general x16, matrix products, per_slot(): jnp.einsum('trab,trcb->trac', weighted, fetched, preferred_element_type=j...  62.4 us
    all_gather x1, waiting for transfers between devices, local(): lax.all_gather(weights, 'space', axis=1, tiled=True)  51.4 us
    dynamic_update_slice x32, local copies, waits for them, and re-layouts, local(): lax.scan(per_slot, jnp.zeros((twists_here, rows, orbit, bands), jnp.float...  42.7 us
    ppermute x1, waiting for transfers between devices, with_halo(): before = lax.ppermute(last, axis, up)  41.5 us
  transfers between devices with their start and end apart: 5, of which 3 were waited for; matrix products, arithmetic and copies ran while one was open for 1% of the time, Pallas kernels for 0%

profile of v1, /device:TPU:0, one launch (start us, length us, event | category | flops | bytes accessed | tf_op | source)
XLA Modules:
  0.0 1060.3 jit_solution(6451055596835501936)
XLA Ops:
  9.6 7.3 collective-permute-start.1
  22.7 41.5 %collective-permute-done = bf16[1,64,64,256]{3,2,1,0:T(8,128)(2,1)} collective-permute-done((bf16[1,64,64,256]{3,2,1,0:T(8,128)(2,1)}, bf16[1,64,64,256]{3,2,1,0:T(8,128)(2,1)}, u32[]{:S(2)}, u32[]{:S(2)}) %collective-permute-start) | collective-permute-done | bytes 2097184 | tf_op jit(solution)/shard_map/ppermute | solution.py:15
  69.7 51.4 %all-gather.4.cloned.1.call-done = bf16[1024,4096]{0,1:T(8,128)(2,1)} async-done(((bf16[1024,64]{0,1:T(8,128)(2,1)}), bf16[1024,4096]{0,1:T(8,128)(2,1)}) %all-gather.4.cloned.1.call-update) | async-done | bytes 8388624 | tf_op jit(solution)/shard_map/all_gather | solution.py:31
  121.1 14.3 %convolution_convert_fusion = bf16[1024,4096]{1,0:T(8,128)(2,1)} fusion(bf16[1024,1024]{1,0:T(8,128)(2,1)S(1)} %bitcast.75, bf16[1024,4096]{0,1:T(8,128)(2,1)} %all-gather.4.cloned.1.call-done), kind=kOutput, calls=%fused_computation.21 | convolution fusion | flops 8594128896 | bytes 18874368 | tf_op jit(solution)/shard_map/dot_general | solution.py:29
  135.4 23.6 %reshape.166 = bf16[1,64,16,64,64]{4,3,2,1,0:T(8,128)(2,1)} reshape(bf16[1024,4096]{1,0:T(8,128)(2,1)} %convolution_convert_fusion) | data formatting | bytes 16777216 | tf_op jit(solution)/shard_map/reshape | solution.py:38
  159.0 14.0 %fusion.15 = bf16[16,1,64,64,64]{4,3,2,1,0:T(8,128)(2,1)} fusion(bf16[1,64,16,64,64]{4,3,2,1,0:T(8,128)(2,1)} %reshape.166, bf16[64,16]{0,1:T(8,128)(2,1)S(1)} %fusion.24), kind=kLoop, calls=%fused_computation.19 | loop fusion | flops 4194304 | bytes 16779264 | tf_op jit(solution)/shard_map/transpose | solution.py:58
  173.0 274.1 %while.13 = (s32[]{:T(128)}, f32[1,64,64,256]{3,2,1,0:T(8,128)}, bf16[16,1,64,64,64]{4,3,2,0,1:T(8,128)(2,1)}, bf16[16,1,64,64,64]{4,3,2,1,0:T(8,128)(2,1)}, s32...) while((s32[]{:T(128)}, f32[1,64,64,256]{3,2,1,0:T(8,128)}, ...), condition=%wide.region_1.2_spmd.clone, body=%wide.region_0.1_spmd.clone.sunk | while | flops 271319552 | bytes 23071752 | solution.py:59
  199.3 5.8 bitcast_add_fusion.2
  216.5 5.8 bitcast_add_fusion.2
  233.7 5.8 bitcast_add_fusion.2
  250.9 5.8 bitcast_add_fusion.2
  268.1 5.8 bitcast_add_fusion.2
  285.3 5.8 bitcast_add_fusion.2
  302.5 5.8 bitcast_add_fusion.2
  337.0 5.8 bitcast_add_fusion.2
  354.2 5.8 bitcast_add_fusion.2
  388.5 5.8 bitcast_add_fusion.2
  405.8 5.8 bitcast_add_fusion.2
  423.0 5.8 bitcast_add_fusion.2
  440.2 5.8 bitcast_add_fusion.2
  447.1 22.6 %reshape.167 = bf16[16,64,4096]{2,1,0:T(8,128)(2,1)} reshape(bf16[16,1,64,64,64]{4,3,2,0,1:T(8,128)(2,1)} %get-tuple-element.46) | data formatting | bytes 16777216 | tf_op jit(solution)/shard_map/reshape.16
  469.7 15.7 %convolution_bitcast_fusion = f32[4096,1024]{1,0:T(8,128)} fusion(bf16[16,64,4096]{2,1,0:T(8,128)(2,1)} %reshape.167, bf16[64,16,1024]{2,1,0:T(8,128)(2,1)S(1)} %bitcast.76), kind=kOutput, calls=%fused_computation.20 | convolution fusion | flops 8589934592 | bytes 27262976 | tf_op jit(solution)/shard_map/strO,trsf->Of/dot_general | solution.py:72
  485.4 392.0 %reduce-scatter.2.cloned.1.call-done = f32[64,1024]{1,0:T(8,128)} async-done(((f32[4096,1024]{1,0:T(8,128)}), f32[64,1024]{1,0:T(8,128)}) %reduce-scatter.2.cloned.1.call-update) | async-done | bytes 262160 | tf_op jit(solution)/shard_map/reduce_scatter | solution.py:71
  880.9 170.6 %all-gather.1 = f32[64,1,256]{2,1,0:T(1,128)S(1)} all-gather(f32[1,1,256]{2,1,0:T(1,128)S(1)} %bitcast.78), channel_id=2, replica_groups=mesh['dp'=2,'space'=64] {'space'}, dimensions={0}, use_global_device_ids=true | all-gather | bytes 66560 | tf_op jit(solution)/shard_map/all_gather | solution.py:65
  (155 shorter events, 217.7 us)
Async XLA Ops:
  7.2 114.0 %copy-start = (bf16[1,64,16,1024]{3,2,1,0:T(8,128)(2,1)S(1)}, bf16[1,64,16,1024]{3,2,1,0:T(8,128)(2,1)}, u32[]{:S(2)}) copy-start(bf16[1,64,16,1024]{3,2,1,0:T(8,128)(2,1)} %param.8) | copy-start | bytes 6291460
  7.2 113.9 %all-gather.4.cloned.1.call-start = ((), (), s32[]{:S(2)}) async-start(), calls=%async_computation.1 | async-start | bytes 8519680 | tf_op jit(solution)/shard_map/all_gather | solution.py:31
  7.9 869.5 %reduce-scatter.2.cloned.1.call-start = ((), (), s32[]{:S(2)}) async-start(), calls=%async_computation.2 | async-start | bytes 17039360 | tf_op jit(solution)/shard_map/reduce_scatter | solution.py:71
  8.0 56.2 %collective-permute-start = (bf16[1,64,64,256]{3,2,1,0:T(8,128)(2,1)}, bf16[1,64,64,256]{3,2,1,0:T(8,128)(2,1)}, u32[]{:S(2)}, u32[]{:S(2)}) collective-permute-start(bf16[1,64,64,256]{3,2,1,0:T(8,128)(2,1)} %param.9), channel_id=1, source_target_pairs={{0,1},{1,2},{2,3},{3,4},{4,5},{5,6},{6,7},{7,8},{8,9},{9,10},{10,1... | collective-permute-start | bytes 6291464 | tf_op jit(solution)/shard_map/ppermute | solution.py:15
  9.6 54.6 %collective-permute-start.1 = (bf16[1,64,64,256]{3,2,1,0:T(8,128)(2,1)}, bf16[1,64,64,256]{3,2,1,0:T(8,128)(2,1)}, u32[]{:S(2)}, u32[]{:S(2)}) collective-permute-start(bf16[1,64,64,256]{3,2,1,0:T(8,128)(2,1)} %param.9), channel_id=1, source_target_pairs={{1,0},{2,1},{3,2},{4,3},{5,4},{6,5},{7,6},{8,7},{9,8},{10,9},{11,1... | collective-permute-start | bytes 6291464 | tf_op jit(solution)/shard_map/ppermute | solution.py:16
  16.9 47.3 %copy-start.1 = (bf16[1,64,64,256]{3,2,1,0:T(8,128)(2,1)S(1)}, bf16[1,64,64,256]{3,2,1,0:T(8,128)(2,1)}, u32[]{:S(2)}) copy-start(bf16[1,64,64,256]{3,2,1,0:T(8,128)(2,1)} %param.9) | copy-start | bytes 6291460
  485.4 566.8 %all-reduce.2.cloned.1.call-start = ((), (), s32[]{:S(2)}) async-start(), calls=%async_computation.3 | async-start | bytes 524288 | tf_op jit(solution)/shard_map/psum | solution.py:77
Sparse Core Ops, SparseCore 0:
  10.9 110.2 all-gather.3
  485.5 391.8 reduce-scatter.1
  879.8 18.4 all-reduce.1
